TPU v7x, 256 devices: a whole 4x4x8 slice. The times are simulated.
256 devices in a mesh: gx: 2 (over core), gy: 4 (over x), gz: 32 (over z, y).
Axes of the slice: x: 4, y: 4, z: 8, core: 2. Of those that a mesh axis runs over, the one named last changes fastest.
Arguments:
- resid_x: float32 [6, 8, 32, 120, 512], P('gx', 'gy', 'gz'), may hold values from -6 to 6
- resid_y: float32 [4, 12, 32, 120, 512], P('gx', 'gy', 'gz'), may hold values from -6 to 6
- face_weights: float32 [4, 8, 32, 4, 120], P('gx', 'gy', 'gz'), may hold values from 0.25 to 0.75
- face_counts: int32 [4, 8, 32, 4], P('gx', 'gy', 'gz'), may hold values from 1 to 4, as said below
- neumann: bfloat16 [4, 8, 32, 480, 480], P('gx', 'gy', 'gz'), may hold values from -0.25 to 0.25
- schur: bfloat16 [4, 8, 32, 480, 480], P('gx', 'gy', 'gz'), may hold values from -0.25 to 0.25
- basis: bfloat16 [4, 8, 32, 480, 64], P('gx', 'gy', 'gz'), may hold values from -0.25 to 0.25
- coarse_map: int32 [4, 8, 32, 64], P('gx', 'gy', 'gz'), may hold values from 0 to 511
- column_inverse: float32 [2, 4, 512, 512], P('gx', 'gy', 'gz'), may hold values from -0.25 to 0.25
- column_basis: float32 [2, 4, 512, 512], P('gx', 'gy', 'gz'), may hold values from -0.25 to 0.25
- top_inverse: float32 [512, 512], replicated, may hold values from -0.09375 to 0.09375
Outputs:
- z_x: float32 [6, 8, 32, 120, 512], P('gx', 'gy', 'gz')
- z_y: float32 [4, 12, 32, 120, 512], P('gx', 'gy', 'gz')
- schur_image: bfloat16 [4, 8, 32, 480, 512], P('gx', 'gy', 'gz')
Inputs may be any that keep to these rules, and one draw needn't show every extreme that they name: `face_counts`: only the first 30 * count of a face's 120 dofs are live; about one face in eight has 4 live mesh faces. `coarse_map`: several local coarse dofs may share a column coarse dof.
All inputs are finite; a program needn't handle non-finite values.
Results may differ from a plain program's by a relative error of at most 0.0063.
Values sent between devices are 32-bit elements; how exact they have to be, the bound alone decides.
No kernel may reach another device: no remote copies, remote signals or barrier semaphores. Data moves between devices by JAX's collectives and lax.ppermute only.
A program may use at most 64 MiB of HBM per device.

v0:
```python
import jax
import jax.numpy as jnp
from jax import lax
from jax.sharding import PartitionSpec as P

BLK = 30


def with_halo(array, sides, width):
    for axis, dim in sides:
        size, length = (lax.axis_size(axis), array.shape[dim])
        up = [(i, (i + 1) % size) for i in range(size)]
        down = [(j, i) for i, j in up]
        last = lax.slice_in_dim(array, length - width, length, axis=dim)
        initial = lax.slice_in_dim(array, 0, width, axis=dim)
        before = lax.ppermute(last, axis, up)
        after = lax.ppermute(initial, axis, down)
        array = jnp.concatenate([before, array, after], axis=dim)
    return array


def assemble_x(copies):
    padded = with_halo(copies, (("gx", 0),), 1)
    return copies + jnp.stack([padded[0], jnp.zeros_like(padded[0]), padded[4]], 0)


def assemble_y(copies):
    padded = with_halo(copies, (("gy", 1),), 1)
    return copies + jnp.stack([padded[:, 0], jnp.zeros_like(padded[:, 0]), padded[:, 4]], 1)


def gather_faces(along_x, along_y):
    return jnp.stack([along_x[0:2], along_x[1:3], along_y[:, 0:2], along_y[:, 1:3]], 2)


def on_device(
    resid_x,
    resid_y,
    face_weights,
    face_counts,
    neumann,
    schur,
    basis,
    coarse_map,
    column_inverse,
    column_basis,
    top_inverse,
):
    high = lax.Precision.HIGHEST
    face_dofs = resid_x.shape[3]
    loads = resid_x.shape[4]
    inner = neumann.shape[3]
    coarse_local = basis.shape[4]
    column_size = column_inverse.shape[3]
    dof_index = jnp.arange(face_dofs, dtype=jnp.int32)
    live = (dof_index[None, None, None, :] < face_counts[:, :, 0, :, None] * BLK).astype(
        jnp.float32
    )
    scale = face_weights[:, :, 0] * live
    assembled_x = assemble_x(resid_x)[:, :, 0]
    assembled_y = assemble_y(resid_y)[:, :, 0]
    faces = gather_faces(assembled_x, assembled_y)
    upart = (faces * scale[..., None]).reshape(4, inner, loads).astype(jnp.bfloat16)
    neumann_flat = neumann.reshape(4, inner, inner)
    basis_flat = basis.reshape(4, inner, coarse_local)
    wpart = jnp.einsum("snk,skr->snr", neumann_flat, upart, preferred_element_type=jnp.float32)
    gpart = jnp.einsum("snc,snr->scr", basis_flat, upart, preferred_element_type=jnp.float32)
    targets = coarse_map.reshape(4 * coarse_local)
    onehot = (targets[:, None] == jnp.arange(column_size, dtype=jnp.int32)[None, :]).astype(
        jnp.float32
    )
    column_part = lax.dot_general(
        onehot, gpart.reshape(4 * coarse_local, loads), (((0,), (0,)), ((), ())), precision=high
    )
    column_res = lax.psum(column_part, "gz")
    inverse_rows = column_inverse[0, 0]
    basis_rows = column_basis[0, 0]
    row_count = inverse_rows.shape[0]
    row_start = lax.axis_index("gz") * row_count
    own_rows = lax.dynamic_slice_in_dim(column_res, row_start, row_count, 0)
    level_two = jnp.dot(inverse_rows, column_res, precision=high)
    top_part = lax.dot_general(basis_rows, own_rows, (((0,), (0,)), ((), ())), precision=high)
    column_top = lax.psum(top_part, "gz")
    top_res = lax.psum(column_top, ("gx", "gy"))
    level_three = jnp.dot(top_inverse, top_res, precision=high)
    value_rows = level_two + jnp.dot(basis_rows, level_three, precision=high)
    column_vals = lax.all_gather(value_rows, "gz", axis=0, tiled=True)
    coarse_vals = (
        jnp.dot(onehot, column_vals, precision=high)
        .reshape(4, coarse_local, loads)
        .astype(jnp.bfloat16)
    )
    ypart = wpart + jnp.einsum(
        "snc,scr->snr", basis_flat, coarse_vals, preferred_element_type=jnp.float32
    )
    contrib = ypart.reshape(2, 2, 4, face_dofs, loads) * scale[..., None]
    send_x = jnp.stack(
        [contrib[0, :, 0], contrib[0, :, 1] + contrib[1, :, 0], contrib[1, :, 1]], 0
    )[:, :, None]
    send_y = jnp.stack(
        [contrib[:, 0, 2], contrib[:, 0, 3] + contrib[:, 1, 2], contrib[:, 1, 3]], 1
    )[:, :, None]
    z_x = assemble_x(send_x)
    z_y = assemble_y(send_y)
    zfaces = gather_faces(z_x[:, :, 0], z_y[:, :, 0])
    zsub = (zfaces * live[..., None]).reshape(4, inner, loads).astype(jnp.bfloat16)
    image = jnp.einsum(
        "snk,skr->snr", schur.reshape(4, inner, inner), zsub, preferred_element_type=jnp.float32
    )
    return (z_x, z_y, image.astype(jnp.bfloat16).reshape(2, 2, 1, inner, loads))


def solution(mesh):
    return jax.shard_map(
        on_device,
        mesh=mesh,
        in_specs=(
            P("gx", "gy", "gz", None, None),
            P("gx", "gy", "gz", None, None),
            P("gx", "gy", "gz", None, None),
            P("gx", "gy", "gz", None),
            P("gx", "gy", "gz", None, None),
            P("gx", "gy", "gz", None, None),
            P("gx", "gy", "gz", None, None),
            P("gx", "gy", "gz", None),
            P("gx", "gy", "gz", None),
            P("gx", "gy", "gz", None),
            P(),
        ),
        out_specs=(
            P("gx", "gy", "gz", None, None),
            P("gx", "gy", "gz", None, None),
            P("gx", "gy", "gz", None, None),
        ),
        check_vma=False,
    )
```

profile of v0, /device:TPU:6, one launch (start us, length us, event | category | flops | bytes accessed | tf_op | source)
XLA Modules:
  0.0 522.4 jit_solution(4546723145671781828)
XLA Ops:
  7.2 2.4 fusion.25
  9.6 2.2 collective-permute-start.2
  11.9 0.8 copy.74
  12.7 0.8 copy.75
  14.6 0.6 reduce.3
  15.8 7.1 %collective-permute-done.2 = f32[2,1,1,120,512]{4,3,1,0,2:T(8,128)} collective-permute-done((f32[2,1,1,120,512]{4,3,1,0,2:T(8,128)}, f32[2,1,1,120,512]{4,3,1,0,2:T(8,128)}, u32[]{:S(2)}, u32[]{:S(2)}) %collective-permute-start.2) | collective-permute-done | bytes 491552 | tf_op jit(solution)/shard_map/ppermute | solution.py:16
  22.9 1.2 collective-permute-done.3
  24.1 1.5 fusion.3
  25.9 1.1 copy-done.6
  27.0 1.5 maximum_add_fusion
  30.2 1.0 copy-done.2
  31.2 1.7 fusion.8
  33.0 153.5 %all-reduce.4.cloned.1.call-done = f32[512,512]{1,0:T(8,128)} async-done(((f32[512,512]{1,0:T(8,128)}), f32[512,512]{1,0:T(8,128)}) %all-reduce.4.cloned.1.call-update) | async-done | bytes 1048592 | tf_op jit(solution)/shard_map/psum | solution.py:75
  186.5 2.8 convolution_bitcast_fusion
  189.4 148.8 %all-reduce.6.cloned.1.call-done = f32[512,512]{0,1:T(8,128)} async-done(((f32[512,512]{0,1:T(8,128)}), f32[512,512]{0,1:T(8,128)}) %all-reduce.6.cloned.1.call-update) | async-done | bytes 1048592 | tf_op jit(solution)/shard_map/psum | solution.py:83
  338.5 0.7 fusion.15
  339.2 64.1 %all-reduce.8.cloned.1.call-done = f32[512,512]{0,1:T(8,128)} async-done(((f32[512,512]{0,1:T(8,128)}), f32[512,512]{0,1:T(8,128)}) %all-reduce.8.cloned.1.call-update) | async-done | bytes 1048592 | tf_op jit(solution)/shard_map/psum | solution.py:84
  403.3 3.4 fusion.26
  406.7 1.6 fusion.5
  408.4 78.2 %all-gather.2.cloned.1.call-done = f32[512,512]{1,0:T(8,128)} async-done(((f32[16,512]{1,0:T(8,128)}), f32[512,512]{1,0:T(8,128)}) %all-gather.2.cloned.1.call-update) | async-done | bytes 1048592 | tf_op jit(solution)/shard_map/all_gather | solution.py:87
  486.6 2.0 convolution_convert_fusion
  488.6 0.7 fusion.27
  489.3 1.4 copy-done.3
  490.7 1.3 convolution_add_fusion
  494.4 1.5 collective-permute-start.7
  496.2 1.3 copy.68
  497.6 9.4 %collective-permute-done.6 = f32[2,1,1,120,512]{4,3,0,2,1:T(8,128)S(1)} collective-permute-done((f32[2,1,1,120,512]{4,3,0,2,1:T(8,128)S(1)}, f32[2,1,1,120,512]{4,3,0,2,1:T(8,128)S(1)}, u32[]{:S(2)}, u32[]{:S(2)}) %collective-permute-start.6) | collective-permute-done | bytes 491552 | tf_op jit(solution)/shard_map/ppermute | solution.py:16
  507.0 1.5 collective-permute-done.7
  510.3 1.0 copy-done.7
  511.3 2.5 fusion.2
  513.8 1.5 fusion.4
  515.3 0.6 copy-done.1
  (72 shorter events, 8.6 us)
Async XLA Ops:
  7.2 482.1 %copy-start = (bf16[2,2,1,480,480]{4,3,2,1,0:T(8,128)(2,1)S(1)}, bf16[2,2,1,480,480]{4,3,2,1,0:T(8,128)(2,1)}, u32[]{:S(2)}) copy-start(bf16[2,2,1,480,480]{4,3,2,1,0:T(8,128)(2,1)} %param.15) | copy-start | bytes 5529604
  7.2 4.6 copy-start.5
  7.2 179.3 %all-reduce.4.cloned.1.call-start = ((), (), s32[]{:S(2)}) async-start(), calls=%async_computation | async-start | bytes 2097152 | tf_op jit(solution)/shard_map/psum | solution.py:75
  9.6 13.3 %collective-permute-start.2 = (f32[2,1,1,120,512]{4,3,1,0,2:T(8,128)}, f32[2,1,1,120,512]{4,3,1,0,2:T(8,128)}, u32[]{:S(2)}, u32[]{:S(2)}) collective-permute-start(f32[2,1,1,120,512]{4,3,1,0,2:T(8,128)} %get-tuple-element.35), channel_id=1, source_target_pairs={{0,32},{32,64},{64,96},{96,0},{1,33},{33,65},{65,97},{97,1},{2,34}... | collective-permute-start | bytes 1474568 | tf_op jit(solution)/shard_map/ppermute | solution.py:16
  11.8 12.3 %collective-permute-start.3 = (f32[2,1,1,120,512]{4,3,1,0,2:T(8,128)}, f32[2,1,1,120,512]{4,3,1,0,2:T(8,128)}, u32[]{:S(2)}, u32[]{:S(2)}) collective-permute-start(f32[2,1,1,120,512]{4,3,1,0,2:T(8,128)} %get-tuple-element.36), channel_id=1, source_target_pairs={{32,0},{64,32},{96,64},{0,96},{33,1},{65,33},{97,65},{1,97},{34,2}... | collective-permute-start | bytes 1474568 | tf_op jit(solution)/shard_map/ppermute | solution.py:17
  11.9 2.2 copy-start.13
  11.9 2.7 copy-start.14
  11.9 3.7 copy-start.12
  11.9 12.2 %copy-start.4 = (f32[2,3,1,120,512]{4,3,2,1,0:T(8,128)S(1)}, f32[2,3,1,120,512]{4,3,2,1,0:T(8,128)}, u32[]{:S(2)}) copy-start(f32[2,3,1,120,512]{4,3,2,1,0:T(8,128)} %param.12) | copy-start | bytes 4423684
  12.7 13.1 %collective-permute-start.1 = (f32[1,2,1,120,512]{4,3,0,1,2:T(8,128)}, f32[1,2,1,120,512]{4,3,0,1,2:T(8,128)}, u32[]{:S(2)}, u32[]{:S(2)}) collective-permute-start(f32[1,2,1,120,512]{4,3,0,1,2:T(8,128)} %copy.74), channel_id=1, source_target_pairs={{128,0},{0,128},{129,1},{1,129},{130,2},{2,130},{131,3},{3,131},{1... | collective-permute-start | bytes 1474568 | tf_op jit(solution)/shard_map/ppermute | solution.py:17
  13.5 12.3 %collective-permute-start = (f32[1,2,1,120,512]{4,3,0,1,2:T(8,128)}, f32[1,2,1,120,512]{4,3,0,1,2:T(8,128)}, u32[]{:S(2)}, u32[]{:S(2)}) collective-permute-start(f32[1,2,1,120,512]{4,3,0,1,2:T(8,128)} %copy.75), channel_id=1, source_target_pairs={{0,128},{128,0},{1,129},{129,1},{2,130},{130,2},{3,131},{131,3},{4... | collective-permute-start | bytes 1474568 | tf_op jit(solution)/shard_map/ppermute | solution.py:16
  25.6 1.4 copy-start.6
  28.7 1.0 copy-start.9
  29.3 1.9 copy-start.2
  31.2 155.3 %copy-start.10 = (f32[1,1,16,512]{3,2,1,0:T(8,128)S(1)}, f32[1,1,16,512]{3,2,1,0:T(8,128)}, u32[]{:S(2)}) copy-start(f32[1,1,16,512]{3,2,1,0:T(8,128)} %param.20) | copy-start | bytes 98308
  32.9 305.4 %all-reduce.6.cloned.1.call-start = ((), (), s32[]{:S(2)}) async-start(), calls=%async_computation.1 | async-start | bytes 2097152 | tf_op jit(solution)/shard_map/psum | solution.py:83
  33.0 305.6 %copy-start.11 = (f32[1,1,16,512]{3,2,1,0:T(8,128)S(1)}, f32[1,1,16,512]{3,2,1,0:T(8,128)}, u32[]{:S(2)}) copy-start(f32[1,1,16,512]{3,2,1,0:T(8,128)} %param.19) | copy-start | bytes 98308
  186.5 152.0 %copy-start.8 = (f32[512,512]{1,0:T(8,128)S(1)}, f32[512,512]{1,0:T(8,128)}, u32[]{:S(2)}) copy-start(f32[512,512]{1,0:T(8,128)} %all-reduce.4.cloned.1.call-done) | copy-start | bytes 3145732
  189.4 213.9 %all-reduce.8.cloned.1.call-start = ((), (), s32[]{:S(2)}) async-start(), calls=%async_computation.2 | async-start | bytes 2097152 | tf_op jit(solution)/shard_map/psum | solution.py:84
  338.3 148.3 %all-gather.2.cloned.1.call-start = ((), (), s32[]{:S(2)}) async-start(), calls=%async_computation.3 | async-start | bytes 1081344 | tf_op jit(solution)/shard_map/all_gather | solution.py:87
  488.5 2.1 copy-start.3
  492.5 3.3 collective-permute-start.5
  492.6 3.2 collective-permute-start.4
  493.7 13.3 %collective-permute-start.6 = (f32[2,1,1,120,512]{4,3,0,2,1:T(8,128)S(1)}, f32[2,1,1,120,512]{4,3,0,2,1:T(8,128)S(1)}, u32[]{:S(2)}, u32[]{:S(2)}) collective-permute-start(f32[2,1,1,120,512]{4,3,0,2,1:T(8,128)S(1)} %get-tuple-element.27), channel_id=1, source_target_pairs={{0,32},{32,64},{64,96},{96,0},{1,33},{33,65},{65,97},{97,1},{2,34}... | collective-permute-start | bytes 1474568 | tf_op jit(solution)/shard_map/ppermute | solution.py:16
  494.4 14.2 %collective-permute-start.7 = (f32[2,1,1,120,512]{4,3,0,2,1:T(8,128)S(1)}, f32[2,1,1,120,512]{4,3,0,2,1:T(8,128)S(1)}, u32[]{:S(2)}, u32[]{:S(2)}) collective-permute-start(f32[2,1,1,120,512]{4,3,0,2,1:T(8,128)S(1)} %get-tuple-element.28), channel_id=1, source_target_pairs={{32,0},{64,32},{96,64},{0,96},{33,1},{65,33},{97,65},{1,97},{34,2}... | collective-permute-start | bytes 1474568 | tf_op jit(solution)/shard_map/ppermute | solution.py:17
  509.7 1.5 copy-start.7
  513.8 2.1 copy-start.1
Sparse Core Ops, SparseCore 0:
  33.0 153.4 all-reduce.3
  190.5 147.6 all-reduce.5
  340.6 62.6 all-reduce.7
  408.4 78.0 all-gather.1
where the time goes:
time: 523 us; the launch traced here: 522 us
  waiting for transfers between devices  464 us (89%)
  matrix products  17.2 us (3%)
  between operations  14.1 us (3%)
  local copies, waits for them, and re-layouts  13.3 us (3%)
  other arithmetic  8.02 us (2%)
  starting transfers between devices  5.73 us (1%)
    psum x1, waiting for transfers between devices, on_device(): column_res = lax.psum(column_part, 'gz')  154 us
    psum x1, waiting for transfers between devices, on_device(): column_top = lax.psum(top_part, 'gz')  149 us
    all_gather x1, waiting for transfers between devices, on_device(): column_vals = lax.all_gather(value_rows, 'gz', axis=0, tiled=True)  78.2 us
    psum x1, waiting for transfers between devices, on_device(): top_res = lax.psum(column_top, ('gx', 'gy'))  64.1 us
    ppermute x4, waiting for transfers between devices, with_halo(): before = lax.ppermute(last, axis, up)  16.6 us
  transfers between devices with their start and end apart: 12, of which 8 were waited for; matrix products, arithmetic and copies ran while one was open for 2% of the time, Pallas kernels for 0%

commit v1 on v0

--- a/solution.py
+++ b/solution.py
@@ -81,7 +81,7 @@
     level_two = jnp.dot(inverse_rows, column_res, precision=high)
     top_part = lax.dot_general(basis_rows, own_rows, (((0,), (0,)), ((), ())), precision=high)
     column_top = lax.psum(top_part, "gz")
-    top_res = lax.psum(column_top, ("gx", "gy"))
+    top_res = lax.psum(lax.psum(column_top, "gx"), "gy")
     level_three = jnp.dot(top_inverse, top_res, precision=high)
     value_rows = level_two + jnp.dot(basis_rows, level_three, precision=high)
     column_vals = lax.all_gather(value_rows, "gz", axis=0, tiled=True)

time: 523 us -> 542 us (1.036)
  waiting for transfers between devices: 464 us -> 483 us
    psum x1 -> x2, waiting for transfers between devices: 64.1 us -> 83.1 us  [on_device(): top_res = lax.psum(lax.psum(column_top, 'gx'), 'gy')]
  transfers between devices with their start and end apart: 12 -> 13, of which waited for: 8 -> 9; matrix products, arithmetic and copies ran while one was open for 2% -> 2% of each run, Pallas kernels for 0% -> 0%
where the time goes in v1:
time: 542 us; the launch traced here: 541 us
  waiting for transfers between devices  483 us (89%)
  matrix products  17.2 us (3%)
  between operations  14.1 us (3%)
  local copies, waits for them, and re-layouts  13.3 us (2%)
  other arithmetic  8.02 us (1%)
  starting transfers between devices  5.77 us (1%)
    psum x1, waiting for transfers between devices, on_device(): column_res = lax.psum(column_part, 'gz')  154 us
    psum x1, waiting for transfers between devices, on_device(): column_top = lax.psum(top_part, 'gz')  149 us
    psum x2, waiting for transfers between devices, on_device(): top_res = lax.psum(lax.psum(column_top, 'gx'), 'gy')  83.1 us
    all_gather x1, waiting for transfers between devices, on_device(): column_vals = lax.all_gather(value_rows, 'gz', axis=0, tiled=True)  78.1 us
    ppermute x4, waiting for transfers between devices, with_halo(): before = lax.ppermute(last, axis, up)  16.6 us
  transfers between devices with their start and end apart: 13, of which 9 were waited for; matrix products, arithmetic and copies ran while one was open for 2% of the time, Pallas kernels for 0%

profile of v1, /device:TPU:6, one launch (start us, length us, event | category | flops | bytes accessed | tf_op | source)
XLA Modules:
  0.0 541.4 jit_solution(12656897857102789408)
XLA Ops:
  7.2 2.4 fusion.25
  9.6 2.2 collective-permute-start.2
  11.9 0.8 copy.74
  12.7 0.8 copy.75
  14.6 0.6 reduce.3
  15.8 7.1 %collective-permute-done.2 = f32[2,1,1,120,512]{4,3,1,0,2:T(8,128)} collective-permute-done((f32[2,1,1,120,512]{4,3,1,0,2:T(8,128)}, f32[2,1,1,120,512]{4,3,1,0,2:T(8,128)}, u32[]{:S(2)}, u32[]{:S(2)}) %collective-permute-start.2) | collective-permute-done | bytes 491552 | tf_op jit(solution)/shard_map/ppermute | solution.py:16
  22.9 1.2 collective-permute-done.3
  24.1 1.5 fusion.3
  25.9 1.1 copy-done.6
  27.0 1.5 maximum_add_fusion
  30.2 1.0 copy-done.2
  31.2 1.7 fusion.8
  33.0 153.6 %all-reduce.5.cloned.1.call-done = f32[512,512]{1,0:T(8,128)} async-done(((f32[512,512]{1,0:T(8,128)}), f32[512,512]{1,0:T(8,128)}) %all-reduce.5.cloned.1.call-update) | async-done | bytes 1048592 | tf_op jit(solution)/shard_map/psum | solution.py:75
  186.5 2.8 convolution_bitcast_fusion
  189.4 148.9 %all-reduce.7.cloned.1.call-done = f32[512,512]{0,1:T(8,128)} async-done(((f32[512,512]{0,1:T(8,128)}), f32[512,512]{0,1:T(8,128)}) %all-reduce.7.cloned.1.call-update) | async-done | bytes 1048592 | tf_op jit(solution)/shard_map/psum | solution.py:83
  338.3 30.0 %all-reduce.9.cloned.1.call-done = f32[512,512]{0,1:T(8,128)} async-done(((f32[512,512]{0,1:T(8,128)}), f32[512,512]{0,1:T(8,128)}) %all-reduce.9.cloned.1.call-update) | async-done | bytes 1048592 | tf_op jit(solution)/shard_map/psum | solution.py:84
  368.6 0.7 fusion.15
  369.2 53.1 %all-reduce.11.cloned.1.call-done = f32[512,512]{0,1:T(8,128)} async-done(((f32[512,512]{0,1:T(8,128)}), f32[512,512]{0,1:T(8,128)}) %all-reduce.11.cloned.1.call-update) | async-done | bytes 1048592 | tf_op jit(solution)/shard_map/psum | solution.py:84
  422.3 3.4 fusion.26
  425.7 1.6 fusion.5
  427.5 78.1 %all-gather.2.cloned.1.call-done = f32[512,512]{1,0:T(8,128)} async-done(((f32[16,512]{1,0:T(8,128)}), f32[512,512]{1,0:T(8,128)}) %all-gather.2.cloned.1.call-update) | async-done | bytes 1048592 | tf_op jit(solution)/shard_map/all_gather | solution.py:87
  505.6 1.9 convolution_convert_fusion
  507.6 0.7 fusion.27
  508.3 1.4 copy-done.3
  509.7 1.3 convolution_add_fusion
  513.4 1.5 collective-permute-start.7
  515.2 1.3 copy.68
  516.6 9.4 %collective-permute-done.6 = f32[2,1,1,120,512]{4,3,0,2,1:T(8,128)S(1)} collective-permute-done((f32[2,1,1,120,512]{4,3,0,2,1:T(8,128)S(1)}, f32[2,1,1,120,512]{4,3,0,2,1:T(8,128)S(1)}, u32[]{:S(2)}, u32[]{:S(2)}) %collective-permute-start.6) | collective-permute-done | bytes 491552 | tf_op jit(solution)/shard_map/ppermute | solution.py:16
  526.1 1.5 collective-permute-done.7
  529.3 1.0 copy-done.7
  530.3 2.5 fusion.2
  532.8 1.5 fusion.4
  (75 shorter events, 9.3 us)
Async XLA Ops:
  7.2 501.1 %copy-start = (bf16[2,2,1,480,480]{4,3,2,1,0:T(8,128)(2,1)S(1)}, bf16[2,2,1,480,480]{4,3,2,1,0:T(8,128)(2,1)}, u32[]{:S(2)}) copy-start(bf16[2,2,1,480,480]{4,3,2,1,0:T(8,128)(2,1)} %param.15) | copy-start | bytes 5529604
  7.2 4.6 copy-start.5
  7.2 179.3 %all-reduce.5.cloned.1.call-start = ((), (), s32[]{:S(2)}) async-start(), calls=%async_computation | async-start | bytes 2097152 | tf_op jit(solution)/shard_map/psum | solution.py:75
  9.6 13.3 %collective-permute-start.2 = (f32[2,1,1,120,512]{4,3,1,0,2:T(8,128)}, f32[2,1,1,120,512]{4,3,1,0,2:T(8,128)}, u32[]{:S(2)}, u32[]{:S(2)}) collective-permute-start(f32[2,1,1,120,512]{4,3,1,0,2:T(8,128)} %get-tuple-element.35), channel_id=1, source_target_pairs={{0,32},{32,64},{64,96},{96,0},{1,33},{33,65},{65,97},{97,1},{2,34}... | collective-permute-start | bytes 1474568 | tf_op jit(solution)/shard_map/ppermute | solution.py:16
  11.8 12.3 %collective-permute-start.3 = (f32[2,1,1,120,512]{4,3,1,0,2:T(8,128)}, f32[2,1,1,120,512]{4,3,1,0,2:T(8,128)}, u32[]{:S(2)}, u32[]{:S(2)}) collective-permute-start(f32[2,1,1,120,512]{4,3,1,0,2:T(8,128)} %get-tuple-element.36), channel_id=1, source_target_pairs={{32,0},{64,32},{96,64},{0,96},{33,1},{65,33},{97,65},{1,97},{34,2}... | collective-permute-start | bytes 1474568 | tf_op jit(solution)/shard_map/ppermute | solution.py:17
  11.9 2.2 copy-start.13
  11.9 2.7 copy-start.14
  11.9 3.7 copy-start.12
  11.9 12.2 %copy-start.4 = (f32[2,3,1,120,512]{4,3,2,1,0:T(8,128)S(1)}, f32[2,3,1,120,512]{4,3,2,1,0:T(8,128)}, u32[]{:S(2)}) copy-start(f32[2,3,1,120,512]{4,3,2,1,0:T(8,128)} %param.12) | copy-start | bytes 4423684
  12.7 13.1 %collective-permute-start.1 = (f32[1,2,1,120,512]{4,3,0,1,2:T(8,128)}, f32[1,2,1,120,512]{4,3,0,1,2:T(8,128)}, u32[]{:S(2)}, u32[]{:S(2)}) collective-permute-start(f32[1,2,1,120,512]{4,3,0,1,2:T(8,128)} %copy.74), channel_id=1, source_target_pairs={{128,0},{0,128},{129,1},{1,129},{130,2},{2,130},{131,3},{3,131},{1... | collective-permute-start | bytes 1474568 | tf_op jit(solution)/shard_map/ppermute | solution.py:17
  13.5 12.3 %collective-permute-start = (f32[1,2,1,120,512]{4,3,0,1,2:T(8,128)}, f32[1,2,1,120,512]{4,3,0,1,2:T(8,128)}, u32[]{:S(2)}, u32[]{:S(2)}) collective-permute-start(f32[1,2,1,120,512]{4,3,0,1,2:T(8,128)} %copy.75), channel_id=1, source_target_pairs={{0,128},{128,0},{1,129},{129,1},{2,130},{130,2},{3,131},{131,3},{4... | collective-permute-start | bytes 1474568 | tf_op jit(solution)/shard_map/ppermute | solution.py:16
  25.6 1.4 copy-start.6
  28.7 1.0 copy-start.9
  29.3 1.9 copy-start.2
  31.2 155.3 %copy-start.10 = (f32[1,1,16,512]{3,2,1,0:T(8,128)S(1)}, f32[1,1,16,512]{3,2,1,0:T(8,128)}, u32[]{:S(2)}) copy-start(f32[1,1,16,512]{3,2,1,0:T(8,128)} %param.20) | copy-start | bytes 98308
  32.9 305.4 %all-reduce.7.cloned.1.call-start = ((), (), s32[]{:S(2)}) async-start(), calls=%async_computation.1 | async-start | bytes 2097152 | tf_op jit(solution)/shard_map/psum | solution.py:83
  189.3 179.3 %copy-start.8 = (f32[512,512]{1,0:T(8,128)S(1)}, f32[512,512]{1,0:T(8,128)}, u32[]{:S(2)}) copy-start(f32[512,512]{1,0:T(8,128)} %all-reduce.5.cloned.1.call-done) | copy-start | bytes 3145732
  189.3 179.3 %copy-start.11 = (f32[1,1,16,512]{3,2,1,0:T(8,128)S(1)}, f32[1,1,16,512]{3,2,1,0:T(8,128)}, u32[]{:S(2)}) copy-start(f32[1,1,16,512]{3,2,1,0:T(8,128)} %param.19) | copy-start | bytes 98308
  189.3 179.0 %all-reduce.9.cloned.1.call-start = ((), (), s32[]{:S(2)}) async-start(), calls=%async_computation.2 | async-start | bytes 2097152 | tf_op jit(solution)/shard_map/psum | solution.py:84
  338.3 84.1 %all-reduce.11.cloned.1.call-start = ((), (), s32[]{:S(2)}) async-start(), calls=%async_computation.3 | async-start | bytes 2097152 | tf_op jit(solution)/shard_map/psum | solution.py:84
  368.3 137.3 %all-gather.2.cloned.1.call-start = ((), (), s32[]{:S(2)}) async-start(), calls=%async_computation.4 | async-start | bytes 1081344 | tf_op jit(solution)/shard_map/all_gather | solution.py:87
  507.6 2.1 copy-start.3
  511.5 3.3 collective-permute-start.5
  511.6 3.2 collective-permute-start.4
  512.8 13.3 %collective-permute-start.6 = (f32[2,1,1,120,512]{4,3,0,2,1:T(8,128)S(1)}, f32[2,1,1,120,512]{4,3,0,2,1:T(8,128)S(1)}, u32[]{:S(2)}, u32[]{:S(2)}) collective-permute-start(f32[2,1,1,120,512]{4,3,0,2,1:T(8,128)S(1)} %get-tuple-element.27), channel_id=1, source_target_pairs={{0,32},{32,64},{64,96},{96,0},{1,33},{33,65},{65,97},{97,1},{2,34}... | collective-permute-start | bytes 1474568 | tf_op jit(solution)/shard_map/ppermute | solution.py:16
  513.4 14.2 %collective-permute-start.7 = (f32[2,1,1,120,512]{4,3,0,2,1:T(8,128)S(1)}, f32[2,1,1,120,512]{4,3,0,2,1:T(8,128)S(1)}, u32[]{:S(2)}, u32[]{:S(2)}) collective-permute-start(f32[2,1,1,120,512]{4,3,0,2,1:T(8,128)S(1)} %get-tuple-element.28), channel_id=1, source_target_pairs={{32,0},{64,32},{96,64},{0,96},{33,1},{65,33},{97,65},{1,97},{34,2}... | collective-permute-start | bytes 1474568 | tf_op jit(solution)/shard_map/ppermute | solution.py:17
  528.7 1.5 copy-start.7
  532.8 2.1 copy-start.1
Sparse Core Ops, SparseCore 0:
  33.0 153.4 all-reduce.4
  190.5 147.6 all-reduce.6
  340.9 27.3 all-reduce.8
  370.5 51.7 all-reduce.10
  427.5 78.0 all-gather.1
